TPU v7x, 256 devices: a whole 4x4x8 slice. The times are simulated.
256 devices in a mesh: wide: 64 (over x, z, core), narrow: 4 (over y).
Axes of the slice: x: 4, y: 4, z: 8, core: 2. Of those that a mesh axis runs over, the one named last changes fastest.
Arguments:
- harvest: bfloat16 [1024, 16384], P('wide', 'narrow'), may hold values from -6 to 6
- pair_ids: int32 [128], P('wide'), may hold values from 0 to 15
- w_enc: bfloat16 [16384, 32768], P('narrow', 'wide'), may hold values from -0.046875 to 0.046875
- b_enc: float32 [32768], P('wide'), may hold values from -3 to 3
- w_dec: bfloat16 [32768, 16384], P('wide', 'narrow'), may hold values from -0.03125 to 0.03125
- b_dec: float32 [16384], P('narrow'), may hold values from -3 to 3
- step_size: float32 [], replicated, may hold values from 0.1 to 0.33
- penalty: float32 [], replicated, may hold values from 0.5 to 2
Outputs:
- latents: float32 [128, 32768], P(None, 'wide')
Inputs may be any that keep to these rules, and one draw needn't show every extreme that they name: Token pair b takes pool row (b // 2) * 16 + pair_ids[b].
All inputs are finite; a program needn't handle non-finite values.
Results may differ from a plain program's by a relative error of at most 0.0025.
Values may be sent and summed in bfloat16 or wider, within the bound.
A program may use at most 64 MiB of HBM per device.

v0:
```python
import jax
import jax.numpy as jnp
from jax import lax
from jax.sharding import PartitionSpec as P

ITERS = 2


def sent_to_all(x, axis):
    length = lax.axis_size(axis)
    return lax.all_to_all(jnp.broadcast_to(x[None], (length, *x.shape)), axis, 0, 0, tiled=True)


def laid_out(blocks, dim):
    blocks = jnp.moveaxis(blocks, 0, dim)
    dims = blocks.shape
    return blocks.reshape(*dims[:dim], dims[dim] * dims[dim + 1], *dims[dim + 2 :])


def gather_directly(x, axis, dim):
    blocks = sent_to_all(x, axis)
    return laid_out(blocks, dim)


def of_everyone(x, axis):
    return sent_to_all(x, axis).sum(axis=0)


def in_one(arrays, axis):
    flat, at, outs = (jnp.concatenate([a.reshape(-1) for a in arrays]), 0, [])
    running = of_everyone(flat, axis)
    for a in arrays:
        outs.append(running[at : at + a.size].reshape(a.shape))
        at += a.size
    return tuple(outs)


def cut_along(x, dim, length):
    dims = x.shape
    blocks = x.reshape(*dims[:dim], length, dims[dim] // length, *dims[dim + 1 :])
    return jnp.moveaxis(blocks, dim, 0)


def sum_at_owner(x, axis, dim):
    blocks = cut_along(x, dim, lax.axis_size(axis))
    arrived = lax.all_to_all(blocks, axis, split_axis=0, concat_axis=0, tiled=True)
    return arrived.astype(jnp.float32).sum(axis=0)


def of_everyone_2(x, axis):
    everything = sent_to_all(x, axis)
    return jnp.sum(everything.astype(jnp.float32), axis=0)


def transpose_product(left, weights):
    return lax.dot_general(
        left, weights, (((1,), (1,)), ((), ())), preferred_element_type=jnp.float32
    )


def local(harvest, pair_ids, w_enc, b_enc, w_dec, b_dec, step_size, penalty):
    pool_rows = harvest.shape[0]
    chooser = (pair_ids[:, None] == jnp.arange(pool_rows, dtype=jnp.int32)[None, :]).astype(
        jnp.bfloat16
    )
    own_pairs = jnp.dot(chooser, harvest, preferred_element_type=jnp.float32).astype(jnp.bfloat16)
    squares = jnp.einsum("ld,ld->l", w_dec, w_dec, preferred_element_type=jnp.float32)
    first_half = lax.axis_index("narrow") < lax.axis_size("narrow") // 2
    square_base = jnp.where(first_half, squares, 0.0)
    square_inst = jnp.where(first_half, 0.0, squares)
    pre_part = jnp.dot(
        gather_directly(own_pairs, "wide", 0), w_enc, preferred_element_type=jnp.float32
    )
    pre, total_base, total_inst = in_one((pre_part, square_base, square_inst), "narrow")
    thresh = penalty * step_size * (jnp.sqrt(total_base) + jnp.sqrt(total_inst))
    latents = jnp.maximum(pre + b_enc, 0.0)
    for step in range(ITERS):
        code_bf = latents.astype(jnp.bfloat16)
        rebuilt = sum_at_owner(
            jnp.dot(code_bf, w_dec, preferred_element_type=jnp.float32).astype(jnp.bfloat16),
            "wide",
            0,
        )
        residual = (own_pairs.astype(jnp.float32) - rebuilt - b_dec).astype(jnp.bfloat16)
        grad_part = transpose_product(gather_directly(residual, "wide", 0), w_dec)
        grad = of_everyone_2(grad_part.astype(jnp.bfloat16), "narrow").astype(jnp.float32)
        latents = jnp.maximum(latents + step_size * grad - thresh, 0.0)
    return latents


def solution(mesh):
    return jax.shard_map(
        local,
        mesh=mesh,
        in_specs=(
            P("wide", "narrow"),
            P("wide"),
            P("narrow", "wide"),
            P("wide"),
            P("wide", "narrow"),
            P("narrow"),
            P(),
            P(),
        ),
        out_specs=P(None, "wide"),
        check_vma=False,
    )
```

profile of v0, /device:TPU:1, one launch (start us, length us, event | category | flops | bytes accessed | tf_op | source)
XLA Modules:
  0.0 254.4 jit_solution(12616916781585231789)
XLA Ops:
  0.0 0.9 copy-done
  0.9 0.9 convolution_convert_fusion.2
  1.8 2.0 broadcast_in_dim.18
  3.8 13.0 %all-to-all-start = ((bf16[64,2,4096]{2,1,0:T(2,128)(2,1)}), bf16[64,2,4096]{2,1,0:T(2,128)(2,1)S(1)}, u32[]{:S(2)}, u32[]{:S(2)}) async-start(bf16[64,2,4096]{2,1,0:T(2,128)(2,1)} %broadcast_in_dim.18), calls=%async_computation | async-start | bytes 2097152 | tf_op jit(solution)/shard_map/all_to_all | solution.py:11
  16.8 3.1 %fusion = f32[512]{0:T(512)S(1)} fusion(bf16[512,4096]{1,0:T(8,128)(2,1)} %param.12), kind=kLoop, calls=%fused_computation.1 | loop fusion | flops 6290944 | bytes 4196352 | tf_op jit(solution)/shard_map/ld,ld->l/dot_general | solution.py:67
  19.9 25.5 %all-to-all-done = bf16[64,2,4096]{2,1,0:T(2,128)(2,1)S(1)} async-done(((bf16[64,2,4096]{2,1,0:T(2,128)(2,1)}), bf16[64,2,4096]{2,1,0:T(2,128)(2,1)S(1)}, u32[]{:S(2)}, u32[]{:S(2)}) %all-to-all-start) | async-done | bytes 1048608 | tf_op jit(solution)/shard_map/all_to_all | solution.py:11
  45.3 0.4 reshape.42
  45.8 2.9 %convolution_bitcast_fusion = f32[16,4,8,128]{3,2,1,0:T(8,128)S(1)} fusion(bf16[128,4096]{1,0:T(8,128)(2,1)S(1)} %reshape.42, bf16[4096,512]{1,0:T(8,128)(2,1)} %param.10), kind=kOutput, calls=%fused_computation.7 | convolution fusion | flops 536870912 | bytes 5505024 | tf_op jit(solution)/shard_map/dot_general | solution.py:71
  48.8 0.5 broadcast_in_dim.20
  49.3 19.0 %all_to_all.41 = f32[4,1,66560]{2,1,0:T(1,128)S(1)} all-to-all(f32[4,1,66560]{2,1,0:T(1,128)S(1)} %broadcast_in_dim.20), channel_id=1, replica_groups=mesh['wide'=64,'narrow'=4] {'narrow'}, dimensions={0} | all-to-all | bytes 2129920 | tf_op jit(solution)/shard_map/all_to_all | solution.py:11
  68.4 1.0 reduce_sum.45
  69.4 2.9 %convolution_convert_fusion.1 = bf16[128,4096]{1,0:T(8,128)(2,1)S(1)} fusion(bf16[512,4096]{1,0:T(8,128)(2,1)} %param.12, f32[128,512]{1,0:T(8,128)S(1)} %slice.20, f32[512]{0:T(512)S(1)} %copy-done.2), kind=kOutput, calls=%fused_computation.3 | convolution fusion | flops 537591808 | bytes 5507072 | tf_op jit(solution)/shard_map/dot_general | solution.py:80
  72.4 0.7 reshape.44
  73.1 35.2 %all_to_all.42 = bf16[64,2,4096]{2,1,0:T(2,128)(2,1)S(1)} all-to-all(bf16[64,2,4096]{2,1,0:T(2,128)(2,1)S(1)} %reshape.44), channel_id=1, replica_groups=mesh['wide'=64,'narrow'=4] {'wide'}, dimensions={0} | all-to-all | bytes 2097152 | tf_op jit(solution)/shard_map/all_to_all | solution.py:46
  108.2 0.9 convert_reduce_fusion.1
  109.1 1.0 broadcast_in_dim.21
  110.1 34.5 %all_to_all.43 = bf16[64,2,4096]{2,1,0:T(2,128)(2,1)S(1)} all-to-all(bf16[64,2,4096]{2,1,0:T(2,128)(2,1)S(1)} %broadcast_in_dim.21), channel_id=1, replica_groups=mesh['wide'=64,'narrow'=4] {'wide'}, dimensions={0} | all-to-all | bytes 2097152 | tf_op jit(solution)/shard_map/all_to_all | solution.py:11
  144.7 0.4 reshape.45
  145.1 3.7 %convolution_convert_fusion.4 = bf16[128,512]{1,0:T(8,128)(2,1)S(1)} fusion(bf16[128,4096]{1,0:T(8,128)(2,1)S(1)} %reshape.45, bf16[512,4096]{1,0:T(8,128)(2,1)} %param.12), kind=kOutput, calls=%fused_computation.9 | convolution fusion | flops 536936448 | bytes 5373952 | tf_op jit(solution)/shard_map/dot_general | solution.py:56
  148.8 0.8 broadcast_in_dim.22
  149.7 3.6 %all-to-all-start.4 = ((bf16[4,128,512]{2,1,0:T(8,128)(2,1)}), bf16[4,128,512]{2,1,0:T(8,128)(2,1)S(1)}, u32[]{:S(2)}, u32[]{:S(2)}) async-start(bf16[4,128,512]{2,1,0:T(8,128)(2,1)} %broadcast_in_dim.22), calls=%async_computation.4 | async-start | bytes 1048576 | tf_op jit(solution)/shard_map/all_to_all | solution.py:11
  154.6 8.1 %all-to-all-done.4 = bf16[4,128,512]{2,1,0:T(8,128)(2,1)S(1)} async-done(((bf16[4,128,512]{2,1,0:T(8,128)(2,1)}), bf16[4,128,512]{2,1,0:T(8,128)(2,1)S(1)}, u32[]{:S(2)}, u32[]{:S(2)}) %all-to-all-start.4) | async-done | bytes 524320 | tf_op jit(solution)/shard_map/all_to_all | solution.py:11
  162.8 2.9 %convolution_convert_fusion = bf16[128,4096]{1,0:T(8,128)(2,1)S(1)} fusion(bf16[512,4096]{1,0:T(8,128)(2,1)} %param.12, f32[128,512]{1,0:T(8,128)S(1)} %convert_reduce_fusion.3, f32[128,512]{1,0:T(8,128)S(1)} %slice.20, f32[512]{0:T(512)S(1)} %fusion.11, f32[]{:T(128)S(6)} %copy.19, f32[512]{0:T(512)S(1)} %copy-done.2), kind=kOutput, calls=%fused_computation.2 | convolution fusion | flops 537853952 | bytes 5771268 | tf_op jit(solution)/shard_map/dot_general | solution.py:80
  165.7 0.7 reshape.46
  166.4 34.8 %all_to_all.44 = bf16[64,2,4096]{2,1,0:T(2,128)(2,1)S(1)} all-to-all(bf16[64,2,4096]{2,1,0:T(2,128)(2,1)S(1)} %reshape.46), channel_id=1, replica_groups=mesh['wide'=64,'narrow'=4] {'wide'}, dimensions={0} | all-to-all | bytes 2097152 | tf_op jit(solution)/shard_map/all_to_all | solution.py:46
  201.2 0.9 convert_reduce_fusion
  202.1 1.0 broadcast_in_dim.23
  203.1 34.5 %all_to_all.45 = bf16[64,2,4096]{2,1,0:T(2,128)(2,1)S(1)} all-to-all(bf16[64,2,4096]{2,1,0:T(2,128)(2,1)S(1)} %broadcast_in_dim.23), channel_id=1, replica_groups=mesh['wide'=64,'narrow'=4] {'wide'}, dimensions={0} | all-to-all | bytes 2097152 | tf_op jit(solution)/shard_map/all_to_all | solution.py:11
  237.7 0.4 reshape.47
  238.1 3.7 %convolution_convert_fusion.3 = bf16[128,512]{1,0:T(8,128)(2,1)S(1)} fusion(bf16[128,4096]{1,0:T(8,128)(2,1)S(1)} %reshape.47, bf16[512,4096]{1,0:T(8,128)(2,1)} %param.12), kind=kOutput, calls=%fused_computation.8 | convolution fusion | flops 536936448 | bytes 5373952 | tf_op jit(solution)/shard_map/dot_general | solution.py:56
  241.9 11.7 %all_to_all.46 = bf16[4,128,512]{2,1,0:T(8,128)(2,1)S(1)} all-to-all(bf16[4,128,512]{2,1,0:T(8,128)(2,1)S(1)} %broadcast_in_dim.24), channel_id=1, replica_groups=mesh['wide'=64,'narrow'=4] {'narrow'}, dimensions={0} | all-to-all | bytes 1048576 | tf_op jit(solution)/shard_map/all_to_all | solution.py:11
  253.6 0.8 subtract_maximum_fusion
  (16 shorter events, 0.4 us)
Async XLA Ops:
  0.0 0.9 copy-start
  3.8 41.5 %all-to-all-start = ((bf16[64,2,4096]{2,1,0:T(2,128)(2,1)}), bf16[64,2,4096]{2,1,0:T(2,128)(2,1)S(1)}, u32[]{:S(2)}, u32[]{:S(2)}) async-start(bf16[64,2,4096]{2,1,0:T(2,128)(2,1)} %broadcast_in_dim.18), calls=%async_computation | async-start | bytes 2097152 | tf_op jit(solution)/shard_map/all_to_all | solution.py:11
  48.7 20.8 %copy-start.2 = (f32[512]{0:T(512)S(1)}, f32[512]{0:T(512)}, u32[]{:S(2)}) copy-start(f32[512]{0:T(512)} %param.11) | copy-start | bytes 6148
  69.4 39.7 %copy-start.1 = (f32[4096]{0:T(1024)S(1)}, f32[4096]{0:T(1024)}, u32[]{:S(2)}) copy-start(f32[4096]{0:T(1024)} %param.13) | copy-start | bytes 49156
  149.7 13.0 %all-to-all-start.4 = ((bf16[4,128,512]{2,1,0:T(8,128)(2,1)}), bf16[4,128,512]{2,1,0:T(8,128)(2,1)S(1)}, u32[]{:S(2)}, u32[]{:S(2)}) async-start(bf16[4,128,512]{2,1,0:T(8,128)(2,1)} %broadcast_in_dim.22), calls=%async_computation.4 | async-start | bytes 1048576 | tf_op jit(solution)/shard_map/all_to_all | solution.py:11
where the time goes:
time: 255 us; the launch traced here: 254 us
  blocking collectives  170 us (67%)
  waiting for transfers between devices  33.5 us (13%)
  matrix products  17 us (7%)
  starting transfers between devices  16.6 us (7%)
  local copies, waits for them, and re-layouts  9.15 us (4%)
  other arithmetic  6.79 us (3%)
    all_to_all x4, blocking collectives, sent_to_all(): lax.all_to_all(jnp.broadcast_to(x[None], (length, *x.shape)), axis, 0, 0,...  99.8 us
    all_to_all x2, blocking collectives, sum_at_owner(): lax.all_to_all(blocks, axis, split_axis=0, concat_axis=0, tiled=True)  70 us
    all_to_all x2, waiting for transfers between devices, sent_to_all(): lax.all_to_all(jnp.broadcast_to(x[None], (length, *x.shape)), axis, 0, 0,...  33.5 us
    all_to_all x2, starting transfers between devices, sent_to_all(): lax.all_to_all(jnp.broadcast_to(x[None], (length, *x.shape)), axis, 0, 0,...  16.6 us
    dot_general x2, matrix products, transpose_product(): lax.dot_general(left, weights, (((1,), (1,)), ((), ())), preferred_elemen...  7.44 us
    dot_general x2, matrix products, local(): jnp.dot(code_bf, w_dec, preferred_element_type=jnp.float32)  5.83 us
    broadcast_in_dim x6, local copies, waits for them, and re-layouts, sent_to_all(): jnp.broadcast_to(x[None], (length, *x.shape))  5.43 us
  transfers between devices with their start and end apart: 2, of which 2 were waited for; matrix products, arithmetic and copies ran while one was open for 1% of the time, Pallas kernels for 0%

commit v1 on v0

v1 whole, which is shorter than its diff:
```python
import functools

import jax
import jax.numpy as jnp
from jax import lax
from jax.experimental import pallas as pl
from jax.experimental.pallas import tpu as pltpu
from jax.sharding import PartitionSpec as P

ITERS = 2
X, Z, C, Y = 4, 8, 2, 4
STREAMS = 2
HALF = 2048
FEAT = 256
LAT = 512
LB = 128
ROWS = 64
PR = 16
MESH = pl.DeviceIdType.MESH
F32, BF16 = jnp.float32, jnp.bfloat16
N_SEMS = 200


def nt(a, b):
    return lax.dot_general(a, b, (((1,), (1,)), ((), ())), preferred_element_type=F32)


def nn(a, b):
    return jnp.dot(a, b, preferred_element_type=F32)


def kernel(ids_ref, step_ref, pen_ref, harvest_hbm, wenc_hbm, benc_ref, wdec_hbm, bdec_ref, out_ref,
           harvest_v, wenc_v, wown_v, woth_v, rows_send, rows_recv, piece_v,
           gpair, gpair_oth, sq_acc, sq_send, sq_recv, pre_send, pre_recv,
           codes, pacc, xsend, xrecv, zsend, zrecv, resid, gsend, grecv, ysend, yrecv, fin,
           local_sems, send_sems, recv_sems):
    w, y = lax.axis_index("wide"), lax.axis_index("narrow")
    x, z, c = w // (Z * C), lax.rem(w // C, Z), lax.rem(w, C)

    def dev(x_, z_, c_, y_):
        return ((x_ * Z + z_) * C + c_, y_)

    def at_x(d):
        return dev(lax.rem(x + d, X), z, c, y)

    def at_z(d):
        return dev(x, lax.rem(z + d, Z), c, y)

    def at_y(d):
        return dev(x, z, c, lax.rem(y + d, Y))

    def at_zc(d):
        i = lax.rem(z * C + c + d, Z * C)
        return dev(x, i // C, lax.rem(i, C), y)

    other = dev(x, z, 1 - c, y)

    n_sems = [0]
    sent = []

    def send(src, dst, device):
        i = n_sems[0]
        n_sems[0] += 1
        copy = pltpu.make_async_remote_copy(
            src_ref=src, dst_ref=dst, send_sem=send_sems.at[i], recv_sem=recv_sems.at[i],
            device_id=device, device_id_type=MESH)
        copy.start()
        sent.append(copy)
        return copy

    loads = [
        pltpu.make_async_copy(harvest_hbm, harvest_v, local_sems.at[0]),
        pltpu.make_async_copy(wenc_hbm, wenc_v, local_sems.at[1]),
        pltpu.make_async_copy(wdec_hbm, wown_v, local_sems.at[2]),
    ]
    loads[0].start()

    barrier = pltpu.get_barrier_semaphore()
    partners = [at_zc(d) for d in range(1, Z * C)] + [at_x(d) for d in range(1, X)] + [at_y(d) for d in range(1, Y)]
    for p in partners:
        pl.semaphore_signal(barrier, inc=1, device_id=p, device_id_type=MESH)
    loads[2].start()
    loads[1].start()

    loads[0].wait()
    row = lax.broadcasted_iota(jnp.int32, (PR, PR), 0)
    col = lax.broadcasted_iota(jnp.int32, (PR, PR), 1)
    wanted = jnp.where(row == 0, ids_ref[0], ids_ref[1])
    chooser = jnp.where((row < 2) & (col == wanted), 1.0, 0.0).astype(BF16)
    for i in range(Z * C):
        f0 = (i % C) * HALF + (i // C) * FEAT
        rows_send[i] = nn(chooser, harvest_v[:, f0:f0 + FEAT])[0:2]
    pl.semaphore_wait(barrier, len(partners))

    me = z * C + c
    row_copies = []
    for d in sorted(range(1, Z * C), key=lambda d: -min(d, Z * C - d)):
        i = lax.rem(me + d, Z * C)
        row_copies.append(send(rows_send.at[i], rows_recv.at[me], at_zc(d)))
    h0 = pl.multiple_of(c * HALF, HALF)
    h1 = pl.multiple_of((1 - c) * HALF, HALF)
    w_copy = send(wdec_hbm.at[:, pl.ds(h1, HALF)], woth_v, other)
    rows_recv[me] = rows_send[me]

    def squares():
        loads[2].wait()

        def body(i, carry):
            r0 = pl.multiple_of(i * PR, PR)
            v = wown_v[pl.ds(r0, PR), :].astype(F32)
            v = v * v
            total = v[:, 0:LB]
            for j in range(1, 2 * HALF // LB):
                total = total + v[:, j * LB:(j + 1) * LB]
            sq_acc[pl.ds(r0, PR), :] = total
            return carry

        lax.fori_loop(0, LAT // PR, body, 0)
        ones = jnp.ones((8, LB), BF16)
        rest, flat = sq_acc[...], jnp.zeros((8, LAT), F32)
        for _ in range(3):
            part = rest.astype(BF16)
            flat = flat + nt(ones, part)
            rest = rest - part.astype(F32)
        for j in range(Y):
            sq_send[j] = flat[:, j * LB:(j + 1) * LB]
        copies = []
        for d in (2, 1, 3):
            copies.append(send(sq_send.at[lax.rem(y + d, Y)], sq_recv.at[y], at_y(d)))
        sq_recv[y] = sq_send[y]
        return copies

    sq_copies = []

    def stream(s):
        if s == 0:
            for cp in row_copies:
                cp.wait_recv()
        rid = lax.broadcasted_iota(jnp.int32, (PR, FEAT), 0)
        piece = jnp.zeros((PR, FEAT), F32)
        for i in range(Z):
            for r in range(2):
                line = jnp.broadcast_to(rows_recv[s * Z + i, r:r + 1, :], (PR, FEAT))
                piece = jnp.where(rid == 2 * i + r, line, piece)
        piece_v[s] = piece
        gpair[s, x, z] = piece.astype(BF16)
        cps = [send(gpair.at[s, x, z], gpair.at[s, x, z], at_z(d)) for d in (4, 3, 5, 2, 6, 1, 7)]
        yield
        for cp in cps:
            cp.wait_recv()
        cps = [send(gpair.at[s, x], gpair.at[s, x], at_x(d)) for d in (2, 1, 3)]
        oth = [send(gpair.at[s, x], gpair_oth.at[s, x], other)]
        yield
        if s == 0:
            sq_copies.extend(squares())
            loads[1].wait()
        for d, cp in zip((2, 1, 3), cps):
            cp.wait_recv()
        for d in (2, 1, 3):
            b = lax.rem(x + d, X)
            oth.append(send(gpair.at[s, b], gpair_oth.at[s, b], other))
        acc = jnp.zeros((ROWS, LAT), F32)
        for k in range(Z):
            f0 = pl.multiple_of(c * HALF + k * FEAT, FEAT)
            acc = acc + nn(gpair[s, :, k].reshape(ROWS, FEAT), wenc_v[pl.ds(f0, FEAT), :])
        yield
        for cp in oth:
            cp.wait_recv()
        for k in range(Z):
            f0 = pl.multiple_of((1 - c) * HALF + k * FEAT, FEAT)
            acc = acc + nn(gpair_oth[s, :, k].reshape(ROWS, FEAT), wenc_v[pl.ds(f0, FEAT), :])
        for j in range(Y):
            pre_send[s, j] = acc[:, j * LB:(j + 1) * LB]
        cps = [send(pre_send.at[s, lax.rem(y + d, Y)], pre_recv.at[s, y], at_y(d)) for d in (2, 1, 3)]
        yield
        if s == 0:
            for cp in sq_copies:
                cp.wait_recv()
        for cp in cps:
            cp.wait_recv()
        norm = jnp.sqrt(sq_recv[0] + sq_recv[1]) + jnp.sqrt(sq_recv[2] + sq_recv[3])
        thresh = pen_ref[0] * step_ref[0] * norm[0:1]
        pre_recv[s, y] = pre_send[s, y]
        pre = (pre_recv[s, 0] + pre_recv[s, 1]) + (pre_recv[s, 2] + pre_recv[s, 3])
        latents = jnp.maximum(pre + benc_ref[y], 0.0)
        for t in range(ITERS):
            codes[t, s, c, y] = latents.astype(BF16)
            own = codes.at[t, s, c, y]
            cps = [send(own, own, at_y(d)) for d in (2, 1, 3)]
            oth = [send(own, own, other)]
            yield
            for d, cp in zip((2, 1, 3), cps):
                cp.wait_recv()
            for d in (2, 1, 3):
                o = codes.at[t, s, c, lax.rem(y + d, Y)]
                oth.append(send(o, o, other))
            code = jnp.concatenate([codes[t, s, c, j] for j in range(Y)], axis=1)
            for k in range(X):
                f0 = pl.multiple_of(c * HALF + k * 512, 512)
                pacc[s, :, k * 512:(k + 1) * 512] = nn(code, wown_v[:, pl.ds(f0, 512)])
            yield
            if s == 0 and t == 0:
                w_copy.wait_recv()
            for cp in oth:
                cp.wait_recv()
            code = jnp.concatenate([codes[t, s, 1 - c, j] for j in range(Y)], axis=1)
            for k in range(X):
                part = pacc[s, :, k * 512:(k + 1) * 512] + nn(code, woth_v[:, k * 512:(k + 1) * 512])
                part = part.astype(BF16)
                for j in range(2):
                    xsend[t, s, :, 2 * k + j] = part[:, j * FEAT:(j + 1) * FEAT].reshape(X, PR, FEAT)
            cps = [send(xsend.at[t, s, lax.rem(x + d, X)], xrecv.at[t, s, d - 1], at_x(d)) for d in (2, 1, 3)]
            yield
            for cp in cps:
                cp.wait_recv()
            for k in range(Z):
                total = xsend[t, s, x, k].astype(F32)
                for d in range(X - 1):
                    total = total + xrecv[t, s, d, k].astype(F32)
                zsend[t, s, k] = total.astype(BF16)
            cps = [send(zsend.at[t, s, lax.rem(z + d, Z)], zrecv.at[t, s, d - 1], at_z(d)) for d in (4, 3, 5, 2, 6, 1, 7)]
            yield
            for cp in cps:
                cp.wait_recv()
            total = zsend[t, s, z].astype(F32)
            for d in range(Z - 1):
                total = total + zrecv[t, s, d].astype(F32)
            resid[t, s, x, z] = (piece_v[s] - total - bdec_ref[me]).astype(BF16)
            own = resid.at[t, s, x, z]
            cps = [send(own, own, at_z(d)) for d in (4, 3, 5, 2, 6, 1, 7)]
            yield
            for cp in cps:
                cp.wait_recv()
            own = resid.at[t, s, x]
            cps = [send(own, own, at_x(d)) for d in (2, 1, 3)]
            yield
            for cp in cps:
                cp.wait_recv()
            acc = jnp.zeros((ROWS, LAT), F32)
            for k in range(Z):
                acc = acc + nt(resid[t, s, :, k].reshape(ROWS, FEAT), woth_v[:, k * FEAT:(k + 1) * FEAT])
            gsend[t, s] = acc
            cp_g = send(gsend.at[t, s], grecv.at[t, s], other)
            acc = jnp.zeros((ROWS, LAT), F32)
            for k in range(Z):
                f0 = pl.multiple_of(c * HALF + k * FEAT, FEAT)
                acc = acc + nt(resid[t, s, :, k].reshape(ROWS, FEAT), wown_v[:, pl.ds(f0, FEAT)])
            yield
            cp_g.wait_recv()
            acc = acc + grecv[t, s]
            for j in range(Y):
                ysend[t, s, j] = acc[:, j * LB:(j + 1) * LB].astype(BF16)
            cps = [send(ysend.at[t, s, lax.rem(y + d, Y)], yrecv.at[t, s, y], at_y(d)) for d in (2, 1, 3)]
            yield
            for cp in cps:
                cp.wait_recv()
            yrecv[t, s, y] = ysend[t, s, y]
            grad = yrecv[t, s, 0].astype(F32)
            for j in range(1, Y):
                grad = grad + yrecv[t, s, j].astype(F32)
            latents = jnp.maximum(latents + step_ref[0] * grad - thresh, 0.0)
        own = fin.at[s, y]
        fin[s, y] = latents
        cps = [send(own, own, at_y(d)) for d in (2, 1, 3)]
        yield
        for cp in cps:
            cp.wait_recv()
        for b in range(X):
            r0 = (b * STREAMS + s) * PR
            for j in range(Y):
                out_ref[r0:r0 + PR, j * LB:(j + 1) * LB] = fin[s, j, b * PR:(b + 1) * PR, :]

    running = [stream(s) for s in range(STREAMS)]
    while running:
        for g in list(running):
            try:
                next(g)
            except StopIteration:
                running.remove(g)
    for cp in sent:
        cp.wait_send()


def local(harvest, pair_ids, w_enc, b_enc, w_dec, b_dec, step_size, penalty):
    vm = pltpu.VMEM
    smem = pl.BlockSpec(memory_space=pltpu.SMEM)
    hbm = pl.BlockSpec(memory_space=pl.ANY)
    vmem = pl.BlockSpec(memory_space=pltpu.VMEM)
    S, T = STREAMS, ITERS
    scratch = [
        vm((16, 2 * HALF), BF16), vm((2 * HALF, LAT), BF16), vm((LAT, 2 * HALF), BF16), vm((LAT, HALF), BF16),
        vm((Z * C, 2, FEAT), F32), vm((Z * C, 2, FEAT), F32), vm((S, PR, FEAT), F32),
        vm((S, X, Z, PR, FEAT), BF16), vm((S, X, Z, PR, FEAT), BF16),
        vm((LAT, LB), F32), vm((Y, 8, LB), F32), vm((Y, 8, LB), F32),
        vm((S, Y, ROWS, LB), F32), vm((S, Y, ROWS, LB), F32),
        vm((T, S, C, Y, ROWS, LB), BF16), vm((S, ROWS, HALF), F32),
        vm((T, S, X, Z, PR, FEAT), BF16), vm((T, S, X - 1, Z, PR, FEAT), BF16),
        vm((T, S, Z, PR, FEAT), BF16), vm((T, S, Z - 1, PR, FEAT), BF16),
        vm((T, S, X, Z, PR, FEAT), BF16),
        vm((T, S, ROWS, LAT), F32), vm((T, S, ROWS, LAT), F32),
        vm((T, S, Y, ROWS, LB), BF16), vm((T, S, Y, ROWS, LB), BF16),
        vm((S, Y, ROWS, LB), F32),
        pltpu.SemaphoreType.DMA((3,)), pltpu.SemaphoreType.DMA((N_SEMS,)), pltpu.SemaphoreType.DMA((N_SEMS,)),
    ]
    b_pieces = b_dec.reshape(C, Z, 1, FEAT).transpose(1, 0, 2, 3).reshape(Z * C, 1, FEAT)
    out = pl.pallas_call(
        kernel,
        out_shape=jax.ShapeDtypeStruct((128, LAT), F32),
        in_specs=[smem, smem, smem, hbm, hbm, vmem, hbm, vmem],
        out_specs=vmem,
        scratch_shapes=scratch,
        compiler_params=pltpu.CompilerParams(collective_id=0, has_side_effects=True, vmem_limit_bytes=56 << 20),
        name="ista",
    )(pair_ids, step_size.reshape(1), penalty.reshape(1), harvest, w_enc, b_enc.reshape(Y, 1, LB), w_dec, b_pieces)
    return out


def solution(mesh):
    return jax.shard_map(
        local,
        mesh=mesh,
        in_specs=(
            P("wide", "narrow"),
            P("wide"),
            P("narrow", "wide"),
            P("wide"),
            P("wide", "narrow"),
            P("narrow"),
            P(),
            P(),
        ),
        out_specs=P(None, "wide"),
        check_vma=False,
    )
```

time: 255 us -> 110 us (0.43)
  blocking collectives: 170 us -> 0 us
  Pallas kernels: 0 us -> 106 us
  waiting for transfers between devices: 33.5 us -> 0 us
  matrix products: 17 us -> 0 us
  starting transfers between devices: 16.6 us -> 0 us
  other arithmetic: 6.79 us -> 0 us
  local copies, waits for them, and re-layouts: 9.15 us -> 3.02 us
    all_to_all x6 -> x0, blocking collectives: 170 us -> none  [the longest x4 99.8 us: sent_to_all(): lax.all_to_all(jnp.broadcast_to(x[None], (length, *x.shape)), axis, 0, 0,...]
    pallas_call x0 -> x1, Pallas kernels: none -> 106 us  [local(): pl.pallas_call(kernel, out_shape=jax.ShapeDtypeStruct((128, LAT), F32), i...]
    all_to_all x2 -> x0, waiting for transfers between devices: 33.5 us -> none  [sent_to_all(): lax.all_to_all(jnp.broadcast_to(x[None], (length, *x.shape)), axis, 0, 0,...]
    dot_general x6 -> x0, matrix products: 17 us -> none  [the longest x2 7.44 us: transpose_product(): lax.dot_general(left, weights, (((1,), (1,)), ((), ())), preferred_elemen...]
    all_to_all x2 -> x0, starting transfers between devices: 16.6 us -> none  [sent_to_all(): lax.all_to_all(jnp.broadcast_to(x[None], (length, *x.shape)), axis, 0, 0,...]
    broadcast_in_dim x6 -> x0, local copies, waits for them, and re-layouts: 5.43 us -> none  [sent_to_all(): jnp.broadcast_to(x[None], (length, *x.shape))]
    dot_general x1 -> x0, other arithmetic: 3.08 us -> none  [local(): jnp.einsum('ld,ld->l', w_dec, w_dec, preferred_element_type=jnp.float32)]
    reduce_sum x5 -> x0, other arithmetic: 2.81 us -> none  [the longest x2 1.7 us: sum_at_owner(): return arrived.astype(jnp.float32).sum(axis=0)]
  transfers between devices with their start and end apart: 2 -> 0, of which waited for: 2 -> 0; matrix products, arithmetic and copies ran while one was open for 1% -> 0% of each run, Pallas kernels for 0% -> 0%
where the time goes in v1:
time: 110 us
  Pallas kernels  106 us (96%)
  local copies, waits for them, and re-layouts  3.02 us (3%)
  between operations  1.31 us (1%)
    pallas_call x1, Pallas kernels, local(): pl.pallas_call(kernel, out_shape=jax.ShapeDtypeStruct((128, LAT), F32), i...  106 us

profile of v1, /device:TPU:1, one launch (start us, length us, event | category | flops | bytes accessed | tf_op | source)
XLA Modules:
  0.0 110.2 jit_solution(13036077634645243710)
XLA Ops:
  1.3 0.7 reshape.18
  2.0 0.6 copy.9
  2.6 105.9 %ista.1 = f32[128,512]{1,0:T(8,128)} custom-call(s32[2]{0:T(128)} %ids_ref.1, f32[1]{0:T(128)} %bitcast.5.step_ref, f32[1]{0:T(128)} %bitcast.6.pen_ref, bf16[16,4096]{1,0:T(8,128)(2,1)} %harvest_hbm.1, bf16[4096,512]{1,0:T(8,128)(2,1)} %wenc_hbm.1, f32[4,1,128]{2,1,0:T(1,128)} %bitcast.9, bf16[512,4096]{1,0:T(8,128)(2,1)} %wdec_hbm.1, f32[16,1,256]{2,1,0:T(1,128)} %bitcast.7), custom_call_target="tpu_custom_call" | custom-call | tf_op jit(solution)/shard_map/ista/pallas_call | solution.py:306
  108.5 1.7 %copy.13 = f32[128,512]{1,0:T(8,128)} copy(f32[128,512]{1,0:T(8,128)} %ista.1) | data formatting | bytes 524288

commit v2 on v0

v2 whole, which is shorter than its diff:
```python
import functools

import jax
import jax.numpy as jnp
from jax import lax
from jax.experimental import pallas as pl
from jax.experimental.pallas import tpu as pltpu
from jax.sharding import PartitionSpec as P

ITERS = 2
X, Z, C, Y = 4, 8, 2, 4
STREAMS = 2
HALF = 2048
FEAT = 256
LAT = 512
LB = 128
ROWS = 64
PR = 16
MESH = pl.DeviceIdType.MESH
F32, BF16 = jnp.float32, jnp.bfloat16
N_SEMS = 260
OFFSET = 4.0
FAR = (4, 3, 5, 2, 6, 1, 7, 0)
NEAR = (0, 1, 7, 2, 6, 3, 5, 4)
PLACE = {d: i for i, d in enumerate(NEAR)}
RUNS = ((0, 1), (1, 3), (3, 5), (5, 7), (7, 8))


def nt(a, b):
    return lax.dot_general(a, b, (((1,), (1,)), ((), ())), preferred_element_type=F32)


def nn(a, b):
    return jnp.dot(a, b, preferred_element_type=F32)


def kernel(ids_ref, step_ref, pen_ref, harvest_hbm, wenc_hbm, benc_ref, wdec_hbm, bdec_ref, out_ref,
           harvest_v, wenc_v, wown_v, woth_v, rows_send, rows_recv,
           wtown_v, wtoth_v, gpair, gpair_oth, sq_acc, sq_all, pre_send, pre_recv, lat, lat_next, acc_v,
           codes, codes_oth, pacc, xsend, xrecv, zsend, zrecv, resid, gsend, grecv, gacc, yall,
           local_sems, send_sems, recv_sems):
    w, y = lax.axis_index("wide"), lax.axis_index("narrow")
    x, z, c = w // (Z * C), lax.rem(w // C, Z), lax.rem(w, C)

    def dev(x_, z_, c_, y_):
        return ((x_ * Z + z_) * C + c_, y_)

    def at_x(d):
        return dev(lax.rem(x + d, X), z, c, y)

    def at_z(d):
        return dev(x, lax.rem(z + d, Z), c, y)

    def at_y(d):
        return dev(x, z, c, lax.rem(y + d, Y))

    def at_zc(d):
        i = lax.rem(z * C + c + d, Z * C)
        return dev(x, i // C, lax.rem(i, C), y)

    other = dev(x, z, 1 - c, y)
    me = z * C + c

    n_sems = [0]
    sent = []

    def send(src, dst, device):
        i = n_sems[0]
        n_sems[0] += 1
        copy = pltpu.make_async_remote_copy(
            src_ref=src, dst_ref=dst, send_sem=send_sems.at[i], recv_sem=recv_sems.at[i],
            device_id=device, device_id_type=MESH)
        copy.start()
        sent.append(copy)
        return copy

    loads = [
        pltpu.make_async_copy(harvest_hbm, harvest_v, local_sems.at[0]),
        pltpu.make_async_copy(wenc_hbm, wenc_v, local_sems.at[1]),
        pltpu.make_async_copy(wdec_hbm, wown_v, local_sems.at[2]),
    ]
    loads[0].start()
    barrier = pltpu.get_barrier_semaphore()
    partners = [at_zc(d) for d in range(1, Z * C)] + [at_x(d) for d in range(1, X)] + [at_y(d) for d in range(1, Y)]
    for p in partners:
        pl.semaphore_signal(barrier, inc=1, device_id=p, device_id_type=MESH)
    loads[2].start()
    loads[1].start()

    loads[0].wait()
    row = lax.broadcasted_iota(jnp.int32, (PR, PR), 0)
    col = lax.broadcasted_iota(jnp.int32, (PR, PR), 1)
    wanted = jnp.where(row == 0, ids_ref[0], ids_ref[1])
    chooser = jnp.where((row < 2) & (col == wanted), 1.0, 0.0).astype(BF16)
    for i in range(C):
        for k in range(4):
            f0 = i * HALF + k * 512
            rows_send[i, :, k * 512:(k + 1) * 512] = nn(chooser, harvest_v[:, f0:f0 + 512])[0:2].astype(BF16)
    pl.semaphore_wait(barrier, len(partners))
    row_copies = []
    for d in sorted(range(1, Z * C), key=lambda d: -min(d, Z * C - d)):
        row_copies.append(send(rows_send.at[lax.rem(c + d, C)], rows_recv.at[me], at_zc(d)))
    h1 = pl.multiple_of((1 - c) * HALF, HALF)
    w_copy = send(wdec_hbm.at[:, pl.ds(h1, HALF)], woth_v, other)
    rows_recv[me] = rows_send[c]

    loads[2].wait()

    def squares(i, carry):
        r0 = pl.multiple_of(i * PR, PR)
        v = wown_v[pl.ds(r0, PR), :].astype(F32)
        v = v * v
        total = v[:, 0:LB]
        for j in range(1, 2 * HALF // LB):
            total = total + v[:, j * LB:(j + 1) * LB]
        sq_acc[pl.ds(r0, PR), :] = total
        return carry

    lax.fori_loop(0, LAT // PR, squares, 0)
    ones = jnp.ones((8, LB), BF16)
    rest, flat = sq_acc[...], jnp.zeros((8, LAT), F32)
    for _ in range(3):
        part = rest.astype(BF16)
        flat = flat + nt(ones, part)
        rest = rest - part.astype(F32)
    sq_all[y] = flat
    sq_copies = [send(sq_all.at[y], sq_all.at[y], at_y(d)) for d in (2, 1, 3)]

    def turned(k, carry):
        f0 = pl.multiple_of(k * FEAT, FEAT)
        wtown_v[pl.ds(f0, FEAT), :] = wown_v[:, pl.ds(pl.multiple_of(c * HALF + k * FEAT, FEAT), FEAT)].T
        return carry

    def turned_oth(k, carry):
        f0 = pl.multiple_of(k * FEAT, FEAT)
        wtoth_v[pl.ds(f0, FEAT), :] = woth_v[:, pl.ds(f0, FEAT)].T
        return carry

    lax.fori_loop(0, Z, turned, 0)

    def stream(s):
        if s == 0:
            for cp in row_copies:
                cp.wait_recv()
        rid = lax.broadcasted_iota(jnp.int32, (8, HALF), 0)
        tops = []
        for top in range(2):
            block = jnp.zeros((8, HALF), F32)
            for i in range(4):
                both = rows_recv[s * Z + top * 4 + i].astype(F32)
                for r in range(2):
                    block = jnp.where(rid == 2 * i + r, jnp.broadcast_to(both[r:r + 1], (8, HALF)), block)
            tops.append(block)
        block = jnp.concatenate(tops, axis=0).astype(BF16)
        for k in range(Z):
            gpair[s, x, k] = block[:, k * FEAT:(k + 1) * FEAT]
        xs, oth = [], []
        for g in (0, 4):
            own = gpair.at[s, x, g:g + 4]
            xs.append([send(own, own, at_x(d)) for d in (2, 1, 3)])
        for g in (0, 4):
            oth.append([send(gpair.at[s, x, g:g + 4], gpair_oth.at[s, x, g:g + 4], other)])
        if s == STREAMS - 1:
            w_copy.wait_recv()
            lax.fori_loop(0, Z, turned_oth, 0)
        yield 0.6, 4.4
        if s == 0:
            loads[1].wait()
        for g in range(2):
            for d, cp in zip((2, 1, 3), xs[g]):
                cp.wait_recv()
                b = lax.rem(x + Y - d, X)
                oth[g].append(send(gpair.at[s, b, 4 * g:4 * g + 4], gpair_oth.at[s, b, 4 * g:4 * g + 4], other))
            for k in range(4 * g, 4 * g + 4):
                f0 = pl.multiple_of(c * HALF + k * FEAT, FEAT)
                part = nn(gpair[s, :, k].reshape(ROWS, FEAT), wenc_v[pl.ds(f0, FEAT), :])
                acc_v[s] = part if k == 0 else acc_v[s] + part
            yield 0.4, 1.4
        for g in range(2):
            for cp in oth[g]:
                cp.wait_recv()
            for k in range(4 * g, 4 * g + 4):
                f0 = pl.multiple_of((1 - c) * HALF + k * FEAT, FEAT)
                acc_v[s] = acc_v[s] + nn(gpair_oth[s, :, k].reshape(ROWS, FEAT), wenc_v[pl.ds(f0, FEAT), :])
        for j in range(Y):
            pre_send[s, j] = acc_v[s, :, j * LB:(j + 1) * LB]
        cps = [send(pre_send.at[s, lax.rem(y + d, Y)], pre_recv.at[s, y], at_y(d)) for d in (2, 1, 3)]
        yield 0.7, 4.5
        for cp in cps:
            cp.wait_recv()
        pre_recv[s, y] = pre_send[s, y]
        pre = (pre_recv[s, 0] + pre_recv[s, 1]) + (pre_recv[s, 2] + pre_recv[s, 3])
        lat[s, y] = jnp.maximum(pre + benc_ref[pl.ds(y, 1), :], 0.0)
        own = lat.at[s, y]
        cps = [send(own, own, at_y(d)) for d in (2, 1, 3)]
        if s == 0:
            for cp in sq_copies:
                cp.wait_recv()
        yield 0.1, 4.5
        for cp in cps:
            cp.wait_recv()
        latents = [lat[s, j] for j in range(Y)]
        for t in range(ITERS):
            code = jnp.concatenate([v.astype(BF16) for v in latents], axis=1)
            codes[t, s] = code
            if t:
                for j in range(Y):
                    lat_next[s, j] = latents[j]
            cp = send(codes.at[t, s], codes_oth.at[t, s], other)
            for i in range(Z):
                k = lax.rem(z + FAR[i], Z)
                f0 = pl.multiple_of(c * HALF + k * FEAT, FEAT)
                pacc[s, i] = nn(code, wown_v[:, pl.ds(f0, FEAT)])
            yield 0.5, 0.6
            cp.wait_recv()
            code = codes_oth[t, s]
            xs = []
            for g in range(4):
                for i in (2 * g, 2 * g + 1):
                    f0 = pl.multiple_of(lax.rem(z + FAR[i], Z) * FEAT, FEAT)
                    part = pacc[s, i] + nn(code, woth_v[:, pl.ds(f0, FEAT)])
                    xsend[t, s, :, i] = part.astype(BF16).reshape(X, PR, FEAT)
                xs.append([send(xsend.at[t, s, lax.rem(x + d, X), 2 * g:2 * g + 2], xrecv.at[t, s, d - 1, 2 * g:2 * g + 2], at_x(d))
                           for d in (2, 1, 3)])
            yield 0.6, 3.2
            zs = []
            for g in range(4):
                for cp in xs[g]:
                    cp.wait_recv()
                for i in (2 * g, 2 * g + 1):
                    total = xsend[t, s, x, i].astype(F32)
                    for d in range(X - 1):
                        total = total + xrecv[t, s, d, i].astype(F32)
                    if FAR[i]:
                        zsend[t, s, i] = total.astype(BF16)
                        zs.append(send(zsend.at[t, s, i], zrecv.at[t, s, i], at_z(FAR[i])))
                if g == 1:
                    yield 0.1, 1.4
            mine = total
            yield 0.1, 3.0
            for i, cp in enumerate(zs):
                cp.wait_recv()
                mine = mine + zrecv[t, s, i].astype(F32)
            b0 = c * (HALF // LB) + z * (FEAT // LB)
            bias = jnp.concatenate([bdec_ref[pl.ds(b0, 1), :], bdec_ref[pl.ds(b0 + 1, 1), :]], axis=1)
            resid[t, s, x, 0] = (gpair[s, x, z].astype(F32) - mine - bias).astype(BF16)
            own = resid.at[t, s, x, 0]
            zs = {d: send(own, resid.at[t, s, x, PLACE[(Z - d) % Z]], at_z(d)) for d in FAR[:-1]}
            xs = []
            for a, b in RUNS:
                if a:
                    for i in range(a, b):
                        zs[(Z - NEAR[i]) % Z].wait_recv()
                run = resid.at[t, s, x, a:b]
                xs.append([send(run, run, at_x(d)) for d in (2, 1, 3)])
                if b in (1, 5):
                    yield 0.2, 2.9
            yield 0.1, 2.6
            for n, (a, b) in enumerate(RUNS):
                for cp in xs[n]:
                    cp.wait_recv()
                for i in range(a, b):
                    k = lax.rem(z + NEAR[i], Z)
                    f0 = pl.multiple_of(k * FEAT, FEAT)
                    part = nn(resid[t, s, :, i].reshape(ROWS, FEAT), wtoth_v[pl.ds(f0, FEAT), :])
                    gsend[t, s] = part if i == 0 else gsend[t, s] + part
                if b == Z:
                    cp = send(gsend.at[t, s], grecv.at[t, s], other)
                for i in range(a, b):
                    k = lax.rem(z + NEAR[i], Z)
                    f0 = pl.multiple_of(k * FEAT, FEAT)
                    part = nn(resid[t, s, :, i].reshape(ROWS, FEAT), wtown_v[pl.ds(f0, FEAT), :])
                    gacc[s] = part if i == 0 else gacc[s] + part
                if b == 5:
                    yield 0.4, 1.6
            yield 0.5, 0.9
            cp.wait_recv()
            yall[t, s, y] = (gacc[s] + grecv[t, s]).astype(BF16)
            own = yall.at[t, s, y]
            cps = [send(own, own, at_y(d)) for d in (2, 1, 3)]
            yield 0.1, 6.0
            for cp in cps:
                cp.wait_recv()
            after = []
            for j in range(Y):
                cols = slice(j * LB, (j + 1) * LB)
                grad = yall[t, s, 0, :, cols].astype(F32)
                for q in range(1, Y):
                    grad = grad + yall[t, s, q, :, cols].astype(F32)
                norm = jnp.sqrt(sq_all[0, 0:1, cols] + sq_all[1, 0:1, cols]) + jnp.sqrt(sq_all[2, 0:1, cols] + sq_all[3, 0:1, cols])
                thresh = pen_ref[0] * step_ref[0] * norm
                after.append((lat_next if t else lat)[s, j] + step_ref[0] * grad - thresh)
            latents = [jnp.maximum(v, 0.0) for v in after]
        for b in range(X):
            r0 = (b * STREAMS + s) * PR
            for j in range(Y):
                out_ref[r0:r0 + PR, j * LB:(j + 1) * LB] = after[j][b * PR:(b + 1) * PR, :]

    now, ready = 0.0, {s: (s * OFFSET, stream(s)) for s in range(STREAMS)}
    while ready:
        s = min(ready, key=lambda k: ready[k][0])
        due, g = ready[s]
        try:
            took, later = next(g)
        except StopIteration:
            del ready[s]
            continue
        now = max(now, due) + took
        ready[s] = (now + later, g)
    for cp in sent:
        cp.wait_send()


def local(harvest, pair_ids, w_enc, b_enc, w_dec, b_dec, step_size, penalty):
    vm = pltpu.VMEM
    smem = pl.BlockSpec(memory_space=pltpu.SMEM)
    hbm = pl.BlockSpec(memory_space=pl.ANY)
    vmem = pl.BlockSpec(memory_space=pltpu.VMEM)
    S, T = STREAMS, ITERS
    scratch = [
        vm((16, 2 * HALF), BF16), vm((2 * HALF, LAT), BF16), vm((LAT, 2 * HALF), BF16), vm((LAT, HALF), BF16),
        vm((C, 2, HALF), BF16), vm((Z * C, 2, HALF), BF16),
        vm((HALF, LAT), BF16), vm((HALF, LAT), BF16),
        vm((S, X, Z, PR, FEAT), BF16), vm((S, X, Z, PR, FEAT), BF16),
        vm((LAT, LB), F32), vm((Y, 8, LAT), F32),
        vm((S, Y, ROWS, LB), F32), vm((S, Y, ROWS, LB), F32), vm((S, Y, ROWS, LB), F32), vm((S, Y, ROWS, LB), F32), vm((S, ROWS, LAT), F32),
        vm((T, S, ROWS, LAT), BF16), vm((T, S, ROWS, LAT), BF16), vm((S, Z, ROWS, FEAT), F32),
        vm((T, S, X, Z, PR, FEAT), BF16), vm((T, S, X - 1, Z, PR, FEAT), BF16),
        vm((T, S, Z, PR, FEAT), BF16), vm((T, S, Z, PR, FEAT), BF16),
        vm((T, S, X, Z, PR, FEAT), BF16),
        vm((T, S, ROWS, LAT), F32), vm((T, S, ROWS, LAT), F32), vm((S, ROWS, LAT), F32),
        vm((T, S, Y, ROWS, LAT), BF16),
        pltpu.SemaphoreType.DMA((3,)), pltpu.SemaphoreType.DMA((N_SEMS,)), pltpu.SemaphoreType.DMA((N_SEMS,)),
    ]
    out = pl.pallas_call(
        kernel,
        out_shape=jax.ShapeDtypeStruct((128, LAT), F32),
        in_specs=[smem, smem, smem, hbm, hbm, vmem, hbm, vmem],
        out_specs=vmem,
        scratch_shapes=scratch,
        compiler_params=pltpu.CompilerParams(collective_id=0, has_side_effects=True, vmem_limit_bytes=56 << 20),
        name="ista",
    )(pair_ids, step_size.reshape(1), penalty.reshape(1), harvest, w_enc, b_enc.reshape(Y, LB), w_dec,
      b_dec.reshape(2 * HALF // LB, LB))
    return jnp.maximum(out, 0.0)


def solution(mesh):
    return jax.shard_map(
        local,
        mesh=mesh,
        in_specs=(
            P("wide", "narrow"),
            P("wide"),
            P("narrow", "wide"),
            P("wide"),
            P("wide", "narrow"),
            P("narrow"),
            P(),
            P(),
        ),
        out_specs=P(None, "wide"),
        check_vma=False,
    )
```

time: 255 us -> 95.7 us (0.38)
  blocking collectives: 170 us -> 0 us
  Pallas kernels: 0 us -> 92.6 us
  waiting for transfers between devices: 33.5 us -> 0 us
  matrix products: 17 us -> 0 us
  starting transfers between devices: 16.6 us -> 0 us
  local copies, waits for them, and re-layouts: 9.15 us -> 0 us
  other arithmetic: 6.79 us -> 1.67 us
    all_to_all x6 -> x0, blocking collectives: 170 us -> none  [the longest x4 99.8 us: sent_to_all(): lax.all_to_all(jnp.broadcast_to(x[None], (length, *x.shape)), axis, 0, 0,...]
    pallas_call x0 -> x1, Pallas kernels: none -> 92.6 us  [local(): pl.pallas_call(kernel, out_shape=jax.ShapeDtypeStruct((128, LAT), F32), i...]
    all_to_all x2 -> x0, waiting for transfers between devices: 33.5 us -> none  [sent_to_all(): lax.all_to_all(jnp.broadcast_to(x[None], (length, *x.shape)), axis, 0, 0,...]
    dot_general x6 -> x0, matrix products: 17 us -> none  [the longest x2 7.44 us: transpose_product(): lax.dot_general(left, weights, (((1,), (1,)), ((), ())), preferred_elemen...]
    all_to_all x2 -> x0, starting transfers between devices: 16.6 us -> none  [sent_to_all(): lax.all_to_all(jnp.broadcast_to(x[None], (length, *x.shape)), axis, 0, 0,...]
    broadcast_in_dim x6 -> x0, local copies, waits for them, and re-layouts: 5.43 us -> none  [sent_to_all(): jnp.broadcast_to(x[None], (length, *x.shape))]
    dot_general x1 -> x0, other arithmetic: 3.08 us -> none  [local(): jnp.einsum('ld,ld->l', w_dec, w_dec, preferred_element_type=jnp.float32)]
    reduce_sum x5 -> x0, other arithmetic: 2.81 us -> none  [the longest x2 1.7 us: sum_at_owner(): return arrived.astype(jnp.float32).sum(axis=0)]
  transfers between devices with their start and end apart: 2 -> 0, of which waited for: 2 -> 0; matrix products, arithmetic and copies ran while one was open for 1% -> 0% of each run, Pallas kernels for 0% -> 0%
where the time goes in v2:
time: 95.7 us; the launch traced here: 95.6 us
  Pallas kernels  92.6 us (97%)
  other arithmetic  1.67 us (2%)
  between operations  1.3 us (1%)
    pallas_call x1, Pallas kernels, local(): pl.pallas_call(kernel, out_shape=jax.ShapeDtypeStruct((128, LAT), F32), i...  92.6 us

profile of v2, /device:TPU:1, one launch (start us, length us, event | category | flops | bytes accessed | tf_op | source)
XLA Modules:
  0.0 95.6 jit_solution(3102030520087804416)
XLA Ops:
  1.3 92.6 %ista.1 = f32[128,512]{1,0:T(8,128)} custom-call(s32[2]{0:T(128)} %ids_ref.1, f32[1]{0:T(128)} %bitcast.4.step_ref, f32[1]{0:T(128)} %bitcast.5.pen_ref, bf16[16,4096]{1,0:T(8,128)(2,1)} %harvest_hbm.1, bf16[4096,512]{1,0:T(8,128)(2,1)} %wenc_hbm.1, f32[4,128]{1,0:T(4,128)} %bitcast.7, bf16[512,4096]{1,0:T(8,128)(2,1)} %wdec_hbm.1, f32[32,128]{1,0:T(8,128)} %bitcast.6), custom_call_target="tpu_custom_call" | custom-call | tf_op jit(solution)/shard_map/ista/pallas_call | solution.py:335
  93.9 1.7 %broadcast_maximum_fusion = f32[128,512]{1,0:T(8,128)} fusion(f32[128,512]{1,0:T(8,128)} %ista.1), kind=kLoop, calls=%fused_computation | loop fusion | flops 65536 | bytes 524288 | tf_op jit(solution)/shard_map/max | solution.py:345

commit v3 on v2

--- a/solution.py
+++ b/solution.py
@@ -160,9 +160,6 @@
             xs.append([send(own, own, at_x(d)) for d in (2, 1, 3)])
         for g in (0, 4):
             oth.append([send(gpair.at[s, x, g:g + 4], gpair_oth.at[s, x, g:g + 4], other)])
-        if s == STREAMS - 1:
-            w_copy.wait_recv()
-            lax.fori_loop(0, Z, turned_oth, 0)
         yield 0.6, 4.4
         if s == 0:
             loads[1].wait()
@@ -185,6 +182,9 @@
         for j in range(Y):
             pre_send[s, j] = acc_v[s, :, j * LB:(j + 1) * LB]
         cps = [send(pre_send.at[s, lax.rem(y + d, Y)], pre_recv.at[s, y], at_y(d)) for d in (2, 1, 3)]
+        if s == 0:
+            w_copy.wait_recv()
+            lax.fori_loop(0, Z, turned_oth, 0)
         yield 0.7, 4.5
         for cp in cps:
             cp.wait_recv()

time: 95.7 us -> 95.8 us (level)
  no operation moved by 1% of the time
where the time goes in v3:
time: 95.8 us; the launch traced here: 95.6 us
  Pallas kernels  92.7 us (97%)
  other arithmetic  1.67 us (2%)
  between operations  1.3 us (1%)
    pallas_call x1, Pallas kernels, local(): pl.pallas_call(kernel, out_shape=jax.ShapeDtypeStruct((128, LAT), F32), i...  92.7 us

profile of v3, /device:TPU:1, one launch (start us, length us, event | category | flops | bytes accessed | tf_op | source)
XLA Modules:
  0.0 95.6 jit_solution(7913988909383196873)
XLA Ops:
  1.3 92.7 %ista.1 = f32[128,512]{1,0:T(8,128)} custom-call(s32[2]{0:T(128)} %ids_ref.1, f32[1]{0:T(128)} %bitcast.4.step_ref, f32[1]{0:T(128)} %bitcast.5.pen_ref, bf16[16,4096]{1,0:T(8,128)(2,1)} %harvest_hbm.1, bf16[4096,512]{1,0:T(8,128)(2,1)} %wenc_hbm.1, f32[4,128]{1,0:T(4,128)} %bitcast.7, bf16[512,4096]{1,0:T(8,128)(2,1)} %wdec_hbm.1, f32[32,128]{1,0:T(8,128)} %bitcast.6), custom_call_target="tpu_custom_call" | custom-call | tf_op jit(solution)/shard_map/ista/pallas_call | solution.py:335
  94.0 1.7 %broadcast_maximum_fusion = f32[128,512]{1,0:T(8,128)} fusion(f32[128,512]{1,0:T(8,128)} %ista.1), kind=kLoop, calls=%fused_computation | loop fusion | flops 65536 | bytes 524288 | tf_op jit(solution)/shard_map/max | solution.py:345
